TPU v7x, 256 devices: a whole 4x4x8 slice. The times are simulated.
256 devices in a mesh: dom: 32 (over y_lo, z, core), repl: 8 (over y_hi, x).
Axes of the slice: x: 4, y: 4 (y_hi: 2, y_lo: 2; y = y_hi * 2 + y_lo), z: 8, core: 2. Of those that a mesh axis runs over, the one named last changes fastest.
Arguments:
- features: float32 [131072, 256], P(('dom', 'repl')), may hold values from -6 to 6
- weight: bfloat16 [256, 256], replicated, may hold values from -0.375 to 0.375
- bias_vector: float32 [256], replicated, may hold values from -0.5 to 0.5
- cotangent: bfloat16 [131072, 256], P(('dom', 'repl')), may hold values from -6 to 6
- near_tiles: bfloat16 [4096, 128, 128], P(('dom', 'repl')), may hold values from -0.1875 to 0.1875
- near_offsets: int32 [256, 33], P(('dom', 'repl')), may hold values from 0 to 16, as said below
- near_cols: int32 [256, 16], P(('dom', 'repl')), may hold values from 0 to 3, as said below
- far_tiles: bfloat16 [256, 32, 1, 128, 128], P(('dom', 'repl')), may hold values from -0.1875 to 0.1875
- far_rows: int32 [256, 32, 1], P(('dom', 'repl')), may hold values from -1 to 31, as said below
- far_cols: int32 [256, 32, 1], P(('dom', 'repl')), may hold values from 0 to 3
Outputs:
- hidden: bfloat16 [131072, 256], P(('dom', 'repl'))
- grad_features: float32 [131072, 256], P(('dom', 'repl'))
- weight_grad: float32 [256, 256], replicated
Inputs may be any that keep to these rules, and one draw needn't show every extreme that they name: `near_offsets`: each row is non-decreasing, begins with 0 and ends with 16. `near_cols`: within one tile row of one device the near tiles' columns differ and rise. `far_rows`: -1 marks an empty slot. A device's slots for the groups whose index of dom lies at most 2 steps from its own around the cycle are never empty.
All inputs are finite; a program needn't handle non-finite values.
Results may differ from a plain program's by a relative error of at most 0.0075.
Values may be sent and summed in bfloat16 or wider, within the bound.
No kernel may reach another device: no remote copies, remote signals or barrier semaphores. Data moves between devices by JAX's collectives and lax.ppermute only.
A program may use at most 128 MiB of HBM per device.

v0:
```python
import math
import jax
import jax.numpy as jnp
from jax import lax
from jax.sharding import PartitionSpec as P


def membership_flags(index, extent, dtype):
    return (index[..., None] == jnp.arange(extent, dtype=jnp.int32)).astype(dtype)


def slot_rows(offsets, slot_count):
    slots = jnp.arange(slot_count, dtype=jnp.int32)
    return jnp.sum((offsets[1:, None] <= slots[None, :]).astype(jnp.int32), axis=0)


def precise_total_sum(form, hot, values):
    return jnp.einsum(form, hot, values, precision=lax.Precision.HIGHEST)


def select(form, hot, values):
    return jnp.einsum(form, hot, values, preferred_element_type=jnp.float32).astype(jnp.bfloat16)


def tile_product(form, tiles, values):
    return jnp.einsum(form, tiles, values, preferred_element_type=jnp.float32)


def activation_grad(pre_values, upstream):
    sigma = jax.nn.sigmoid(pre_values)
    return (upstream.astype(jnp.float32) * sigma * (1.0 + pre_values * (1.0 - sigma))).astype(
        jnp.bfloat16
    )


def on_device(
    features,
    weight,
    bias_vector,
    cotangent,
    near_tiles,
    near_offsets,
    near_cols,
    far_tiles,
    far_rows,
    far_cols,
):
    rows_dev, feat_width = features.shape
    tile_size = near_tiles.shape[1]
    blocks_per_processor = rows_dev // tile_size
    dom_count = lax.axis_size("dom")
    repl_count = lax.axis_size("repl")
    blocks_dom = blocks_per_processor * repl_count
    near_count = near_tiles.shape[0]
    far_block = far_tiles[0]
    far_row_ids = far_rows[0]
    far_col_ids = far_cols[0]
    near_row_ids = slot_rows(near_offsets[0], near_count)
    nearby_column_index = near_cols[0]
    reduced = features.astype(jnp.bfloat16)
    local_block_list = reduced.reshape(blocks_per_processor, tile_size, feat_width)
    nearby_input_rows = select(
        "el,lxh->exh",
        membership_flags(nearby_column_index, blocks_per_processor, jnp.bfloat16),
        local_block_list,
    )
    near_prod = tile_product("qab,qbf->qaf", near_tiles, nearby_input_rows)
    partial_sum = precise_total_sum(
        "qr,qaf->raf", membership_flags(near_row_ids, blocks_dom, jnp.float32), near_prod
    )
    shard_rows = lax.all_gather(reduced, "dom", axis=0, tiled=True)
    range_count = shard_rows.shape[0] // rows_dev
    tiles = far_block
    row_ids = far_row_ids
    col_ids = far_col_ids
    source = shard_rows.reshape(range_count, blocks_per_processor, tile_size, feat_width)
    inputs = select(
        "kqc,kcbf->kqbf", membership_flags(col_ids, blocks_per_processor, jnp.bfloat16), source
    )
    far_prod = tile_product("kqab,kqbf->kqaf", tiles, inputs)
    partial_sum = partial_sum + precise_total_sum(
        "kqr,kqaf->raf", membership_flags(row_ids, blocks_dom, jnp.float32), far_prod
    )
    group_partial = partial_sum.reshape(blocks_dom * tile_size, feat_width)
    summed = lax.psum_scatter(group_partial, "repl", scatter_dimension=0, tiled=True).astype(
        jnp.bfloat16
    )
    pre_act = jnp.dot(summed, weight, preferred_element_type=jnp.float32) + bias_vector
    hidden = jax.nn.silu(pre_act).astype(jnp.bfloat16)
    grad_pre = activation_grad(pre_act, cotangent)
    weight_term = lax.dot_general(
        summed, grad_pre, (((0,), (0,)), ((), ())), preferred_element_type=jnp.float32
    )
    grad_rows = lax.dot_general(
        grad_pre, weight, (((1,), (1,)), ((), ())), preferred_element_type=jnp.float32
    ).astype(jnp.bfloat16)
    group_grad = lax.all_gather(grad_rows, "repl", axis=0, tiled=True)
    node_total = rows_dev * dom_count * repl_count
    weight_grad = lax.psum(weight_term, ("dom", "repl")) * (1.0 / math.sqrt(node_total))
    cluster_block_list = group_grad.reshape(blocks_dom, tile_size, feat_width)
    near_grads = select(
        "om,mgh->ogh", membership_flags(near_row_ids, blocks_dom, jnp.bfloat16), cluster_block_list
    )
    nearby_backward_pass = tile_product("ltp,ltk->lpk", near_tiles, near_grads)
    local_contribution = precise_total_sum(
        "ml,mrx->lrx",
        membership_flags(nearby_column_index, blocks_per_processor, jnp.float32),
        nearby_backward_pass,
    )
    row_count = rows_dev * lax.axis_size("dom")
    tiles = far_block
    row_ids = far_row_ids
    col_ids = far_col_ids
    far_grads = select(
        "kqr,rbf->kqbf", membership_flags(row_ids, blocks_dom, jnp.bfloat16), cluster_block_list
    )
    terms = tile_product("kqab,kqaf->kqbf", tiles, far_grads)
    placed = precise_total_sum(
        "kqc,kqbf->kcbf", membership_flags(col_ids, blocks_per_processor, jnp.float32), terms
    )
    far_grad = lax.psum_scatter(
        placed.reshape(row_count, feat_width).astype(jnp.bfloat16),
        "dom",
        scatter_dimension=0,
        tiled=True,
    ).astype(jnp.float32)
    grad_features = far_grad + local_contribution.reshape(rows_dev, feat_width)
    return (hidden, grad_features, weight_grad)


def solution(mesh):
    placed = (
        P(("dom", "repl"), None),
        P(),
        P(),
        P(("dom", "repl"), None),
        P(("dom", "repl"), None, None),
        P(("dom", "repl"), None),
        P(("dom", "repl"), None),
        P(("dom", "repl"), None, None, None, None),
        P(("dom", "repl"), None, None),
        P(("dom", "repl"), None, None),
    )
    return jax.shard_map(
        on_device,
        mesh=mesh,
        in_specs=placed,
        out_specs=(P(("dom", "repl"), None), P(("dom", "repl"), None), P()),
        check_vma=False,
    )
```

profile of v0, /device:TPU:2, one launch (start us, length us, event | category | flops | bytes accessed | tf_op | source)
XLA Modules:
  0.0 674.9 jit_solution(15560080894403100846)
XLA Ops:
  7.2 1.9 convert_element_type.53
  10.7 1.9 convolution_bitcast_fusion.3
  12.6 2.3 copy.19
  15.2 3.6 fusion.28
  18.7 66.3 %all-gather.3.cloned.1.call-done = bf16[16384,256]{1,0:T(8,128)(2,1)} async-done(((bf16[512,256]{1,0:T(8,128)(2,1)}), bf16[16384,256]{1,0:T(8,128)(2,1)}) %all-gather.3.cloned.1.call-update) | async-done | bytes 8388624 | tf_op jit(solution)/shard_map/all_gather | solution.py:71
  85.0 11.8 %fusion = bf16[32,1,128,256]{3,1,2,0:T(2,128)(2,1)} fusion(bf16[32,4,128,256]{3,2,1,0:T(8,128)(2,1)} %bitcast.65, pred[32,4,1,1]{1,0,2,3:T(32,128)(4,1)S(1)} %get-tuple-element.6), kind=kOutput, calls=%fused_computation.1 | convolution fusion | flops 8388608 | bytes 10485888 | tf_op jit(solution)/shard_map/kqc,kcbf->kqbf/dot_general | solution.py:22
  96.8 8.6 %copy.31 = bf16[32,1,128,256]{2,3,0,1:T(8,128)(2,1)S(1)} copy(bf16[32,1,128,256]{3,1,2,0:T(2,128)(2,1)} %fusion) | data formatting | bytes 4194304 | tf_op jit(solution)/shard_map/kqc,kcbf->kqbf/dot_general | solution.py:22
  105.4 2.7 convolution_bitcast_fusion.1
  108.1 5.5 copy.20
  113.6 5.7 convolution_add_fusion
  119.3 4.4 copy.21
  123.8 89.6 %reduce-scatter.3.cloned.1.call-done = f32[512,256]{1,0:T(8,128)} async-done(((f32[4096,256]{1,0:T(8,128)}), f32[512,256]{1,0:T(8,128)}) %reduce-scatter.3.cloned.1.call-update) | async-done | bytes 524304 | tf_op jit(solution)/shard_map/reduce_scatter | solution.py:85
  213.4 2.2 multiply_convert_fusion.1
  218.0 57.9 %all-gather.5.cloned.1.call-done = bf16[4096,256]{1,0:T(8,128)(2,1)} async-done(((bf16[512,256]{1,0:T(8,128)(2,1)}), bf16[4096,256]{1,0:T(8,128)(2,1)}) %all-gather.5.cloned.1.call-update) | async-done | bytes 2097168 | tf_op jit(solution)/shard_map/all_gather | solution.py:97
  275.8 2.9 convolution_convert_fusion
  278.8 3.7 convolution_bitcast_fusion
  282.5 5.6 copy.24
  288.1 8.7 %multiply_convert_fusion = bf16[32,4,128,256]{3,2,1,0:T(8,128)(2,1)} fusion(f32[32,128,256]{2,1,0:T(8,128)} %copy.24, f32[32,4]{1,0:T(8,128)S(1)} %get-tuple-element.5), kind=kLoop, calls=%fused_computation | loop fusion | flops 8388608 | bytes 12583424 | tf_op jit(solution)/shard_map/convert_element_type | solution.py:122
  296.8 238.4 %all-reduce.2.cloned.1.call-done = f32[256,256]{1,0:T(8,128)} async-done(((f32[256,256]{1,0:T(8,128)}), f32[256,256]{1,0:T(8,128)}) %all-reduce.2.cloned.1.call-update) | async-done | bytes 262160 | tf_op jit(solution)/shard_map/psum | solution.py:99
  535.2 1.7 broadcast_multiply_fusion
  538.7 2.0 copy.27
  540.8 2.4 fusion.33
  543.3 123.3 %reduce-scatter.5.cloned.1.call-done = bf16[512,256]{1,0:T(8,128)(2,1)} async-done(((bf16[16384,256]{1,0:T(8,128)(2,1)}), bf16[512,256]{1,0:T(8,128)(2,1)}) %reduce-scatter.5.cloned.1.call-update) | async-done | bytes 262160 | tf_op jit(solution)/shard_map/reduce_scatter | solution.py:121
  666.6 1.8 bitcast_add_fusion
  (43 shorter events, 6.1 us)
Async XLA Ops:
  7.2 98.3 %copy-start = (bf16[1,32,1,128,128]{4,3,2,1,0:T(8,128)(2,1)S(1)}, bf16[1,32,1,128,128]{4,3,2,1,0:T(8,128)(2,1)}, u32[]{:S(2)}) copy-start(bf16[1,32,1,128,128]{4,3,2,1,0:T(8,128)(2,1)} %param.17) | copy-start | bytes 3145732
  7.2 3.5 copy-start.2
  7.2 77.8 %all-gather.3.cloned.1.call-start = ((), (), s32[]{:S(2)}) async-start(), calls=%async_computation.2 | async-start | bytes 8650752 | tf_op jit(solution)/shard_map/all_gather | solution.py:71
  9.2 204.3 %reduce-scatter.3.cloned.1.call-start = ((), (), s32[]{:S(2)}) async-start(), calls=%async_computation.3 | async-start | bytes 4718592 | tf_op jit(solution)/shard_map/reduce_scatter | solution.py:85
  12.6 2.3 copy-start.11
  12.6 2.5 copy-start.8
  108.1 5.5 copy-start.6
  123.7 89.7 %copy-start.5 = (bf16[256,256]{1,0:T(8,128)(2,1)S(1)}, bf16[256,256]{1,0:T(8,128)(2,1)}, u32[]{:S(2)}) copy-start(bf16[256,256]{1,0:T(8,128)(2,1)} %param.11) | copy-start | bytes 393220
  123.7 89.7 %copy-start.9 = (bf16[512,256]{1,0:T(8,128)(2,1)S(1)}, bf16[512,256]{1,0:T(8,128)(2,1)}, u32[]{:S(2)}) copy-start(bf16[512,256]{1,0:T(8,128)(2,1)} %param.13) | copy-start | bytes 786436
  123.7 89.7 %copy-start.10 = (f32[256]{0:T(256)S(1)}, f32[256]{0:T(256)}, u32[]{:S(2)}) copy-start(f32[256]{0:T(256)} %param.12) | copy-start | bytes 3076
  123.7 152.1 %all-gather.5.cloned.1.call-start = ((), (), s32[]{:S(2)}) async-start(), calls=%async_computation.4 | async-start | bytes 2359296 | tf_op jit(solution)/shard_map/all_gather | solution.py:97
  213.4 3.5 copy-start.4
  216.7 318.5 %all-reduce.2.cloned.1.call-start = ((), (), s32[]{:S(2)}) async-start(), calls=%async_computation.6 | async-start | bytes 524288 | tf_op jit(solution)/shard_map/psum | solution.py:99
  217.9 448.7 %reduce-scatter.5.cloned.1.call-start = ((), (), s32[]{:S(2)}) async-start(), calls=%async_computation.5 | async-start | bytes 8650752 | tf_op jit(solution)/shard_map/reduce_scatter | solution.py:121
  296.8 240.1 %copy-start.1 = (bf16[4096,256]{1,0:T(8,128)(2,1)S(1)}, bf16[4096,256]{1,0:T(8,128)(2,1)}, u32[]{:S(2)}) copy-start(bf16[4096,256]{1,0:T(8,128)(2,1)} %all-gather.5.cloned.1.call-done) | copy-start | bytes 6291460
  535.2 3.0 copy-start.3
  538.7 2.0 copy-start.7
Sparse Core Ops, SparseCore 0:
  10.4 74.5 all-gather.2
  123.9 89.5 reduce-scatter.2
  216.8 59.0 all-gather.4
  281.7 253.4 all-reduce.1
  537.6 128.9 reduce-scatter.4
where the time goes:
time: 676 us; the launch traced here: 675 us
  waiting for transfers between devices  576 us (85%)
  matrix products  42.2 us (6%)
  local copies, waits for them, and re-layouts  28.6 us (4%)
  other arithmetic  14.4 us (2%)
  between operations  13.9 us (2%)
    psum x1, waiting for transfers between devices, on_device(): lax.psum(weight_term, ('dom', 'repl')) * (1.0 / math.sqrt(node_total))  238 us
    reduce_scatter x1, waiting for transfers between devices, on_device(): lax.psum_scatter(placed.reshape(row_count, feat_width).astype(jnp.bfloat1...  123 us
    reduce_scatter x1, waiting for transfers between devices, on_device(): lax.psum_scatter(group_partial, 'repl', scatter_dimension=0, tiled=True)  89.6 us
    all_gather x1, waiting for transfers between devices, on_device(): shard_rows = lax.all_gather(reduced, 'dom', axis=0, tiled=True)  66.3 us
    all_gather x1, waiting for transfers between devices, on_device(): group_grad = lax.all_gather(grad_rows, 'repl', axis=0, tiled=True)  57.9 us
    dot_general x4, matrix products, select(): jnp.einsum(form, hot, values, preferred_element_type=jnp.float32)  17.5 us
    dot_general x4, local copies, waits for them, and re-layouts, tile_product(): return jnp.einsum(form, tiles, values, preferred_element_type=jnp.float32)  15.4 us
  transfers between devices with their start and end apart: 5, of which 5 were waited for; matrix products, arithmetic and copies ran while one was open for 6% of the time, Pallas kernels for 0%

commit v1 on v0

--- a/solution.py
+++ b/solution.py
@@ -96,7 +96,9 @@
     ).astype(jnp.bfloat16)
     group_grad = lax.all_gather(grad_rows, "repl", axis=0, tiled=True)
     node_total = rows_dev * dom_count * repl_count
-    weight_grad = lax.psum(weight_term, ("dom", "repl")) * (1.0 / math.sqrt(node_total))
+    weight_grad = jnp.sum(lax.all_gather(weight_term, ("dom", "repl")), axis=0) * (
+        1.0 / math.sqrt(node_total)
+    )
     cluster_block_list = group_grad.reshape(blocks_dom, tile_size, feat_width)
     near_grads = select(
         "om,mgh->ogh", membership_flags(near_row_ids, blocks_dom, jnp.bfloat16), cluster_block_list

time: 676 us -> 1250 us (1.85)
  waiting for transfers between devices: 576 us -> 1120 us
  other arithmetic: 14.4 us -> 34.5 us
    all_gather x0 -> x1, waiting for transfers between devices: none -> 786 us  [on_device(): lax.all_gather(weight_term, ('dom', 'repl'))]
    psum x1 -> x0, waiting for transfers between devices: 238 us -> none  [on_device(): lax.psum(weight_term, ('dom', 'repl')) * (1.0 / math.sqrt(node_total))]
    reduce_sum x0 -> x1, other arithmetic: none -> 21.1 us  [on_device(): jnp.sum(lax.all_gather(weight_term, ('dom', 'repl')), axis=0)]
  transfers between devices with their start and end apart: 5 -> 5, of which waited for: 5 -> 5; matrix products, arithmetic and copies ran while one was open for 6% -> 2% of each run, Pallas kernels for 0% -> 0%
where the time goes in v1:
time: 1250 us; the launch traced here: 1240 us
  waiting for transfers between devices  1120 us (90%)
  matrix products  43.1 us (3%)
  other arithmetic  34.5 us (3%)
  local copies, waits for them, and re-layouts  29.5 us (2%)
  between operations  13.9 us (1%)
    all_gather x1, waiting for transfers between devices, on_device(): lax.all_gather(weight_term, ('dom', 'repl'))  786 us
    reduce_scatter x1, waiting for transfers between devices, on_device(): lax.psum_scatter(placed.reshape(row_count, feat_width).astype(jnp.bfloat1...  120 us
    reduce_scatter x1, waiting for transfers between devices, on_device(): lax.psum_scatter(group_partial, 'repl', scatter_dimension=0, tiled=True)  89.7 us
    all_gather x1, waiting for transfers between devices, on_device(): shard_rows = lax.all_gather(reduced, 'dom', axis=0, tiled=True)  66.3 us
    all_gather x1, waiting for transfers between devices, on_device(): group_grad = lax.all_gather(grad_rows, 'repl', axis=0, tiled=True)  59 us
  transfers between devices with their start and end apart: 5, of which 5 were waited for; matrix products, arithmetic and copies ran while one was open for 2% of the time, Pallas kernels for 0%

profile of v1, /device:TPU:2, one launch (start us, length us, event | category | flops | bytes accessed | tf_op | source)
XLA Modules:
  0.0 1242.0 jit_solution(6981419942553817055)
XLA Ops:
  7.2 1.9 convert_element_type.53
  10.7 1.9 convolution_bitcast_fusion.3
  12.6 2.3 copy.19
  15.2 3.6 fusion.28
  18.7 66.3 %all-gather.5.cloned.1.call-done = bf16[16384,256]{1,0:T(8,128)(2,1)} async-done(((bf16[512,256]{1,0:T(8,128)(2,1)}), bf16[16384,256]{1,0:T(8,128)(2,1)}) %all-gather.5.cloned.1.call-update) | async-done | bytes 8388624 | tf_op jit(solution)/shard_map/all_gather | solution.py:71
  85.0 11.8 fusion
  96.8 8.6 copy.31
  105.4 2.7 convolution_bitcast_fusion.1
  108.1 5.5 copy.20
  113.6 5.7 convolution_add_fusion
  119.3 4.4 copy.21
  123.8 89.7 %reduce-scatter.3.cloned.1.call-done = f32[512,256]{1,0:T(8,128)} async-done(((f32[4096,256]{1,0:T(8,128)}), f32[512,256]{1,0:T(8,128)}) %reduce-scatter.3.cloned.1.call-update) | async-done | bytes 524304 | tf_op jit(solution)/shard_map/reduce_scatter | solution.py:85
  213.5 2.2 multiply_convert_fusion.1
  216.8 59.0 %all-gather.7.cloned.1.call-done = bf16[4096,256]{1,0:T(8,128)(2,1)} async-done(((bf16[512,256]{1,0:T(8,128)(2,1)}), bf16[4096,256]{1,0:T(8,128)(2,1)}) %all-gather.7.cloned.1.call-update) | async-done | bytes 2097168 | tf_op jit(solution)/shard_map/all_gather | solution.py:97
  275.8 2.9 convolution_convert_fusion
  278.7 3.7 convolution_bitcast_fusion
  282.5 5.6 copy.24
  288.1 8.7 multiply_convert_fusion
  301.7 2.0 copy.27
  303.7 2.4 fusion.33
  306.2 120.1 %reduce-scatter.5.cloned.1.call-done = bf16[512,256]{1,0:T(8,128)(2,1)} async-done(((bf16[16384,256]{1,0:T(8,128)(2,1)}), bf16[512,256]{1,0:T(8,128)(2,1)}) %reduce-scatter.5.cloned.1.call-update) | async-done | bytes 262160 | tf_op jit(solution)/shard_map/reduce_scatter | solution.py:123
  426.3 1.8 bitcast_add_fusion
  428.1 785.6 %all-gather.9.cloned.1.call-done = f32[65536,256]{1,0:T(8,128)} async-done(((f32[256,256]{1,0:T(8,128)}), f32[65536,256]{1,0:T(8,128)}) %all-gather.9.cloned.1.call-update) | async-done | bytes 67108880 | tf_op jit(solution)/shard_map/all_gather | solution.py:99
  1213.7 21.1 %reduce_sum.19 = f32[256,256]{1,0:T(8,128)S(1)} reduce(f32[256,256,256]{2,1,0:T(8,128)} %bitcast.22, f32[]{:T(128)} %constant.2.clone.1), dimensions={0}, to_apply=%region_3.4 | reduce | flops 16711680 | bytes 67371008 | tf_op jit(solution)/shard_map/reduce_sum | solution.py:99
  (44 shorter events, 8.8 us)
Async XLA Ops:
  7.2 98.3 %copy-start = (bf16[1,32,1,128,128]{4,3,2,1,0:T(8,128)(2,1)S(1)}, bf16[1,32,1,128,128]{4,3,2,1,0:T(8,128)(2,1)}, u32[]{:S(2)}) copy-start(bf16[1,32,1,128,128]{4,3,2,1,0:T(8,128)(2,1)} %param.17) | copy-start | bytes 3145732
  7.2 3.5 copy-start.3
  7.2 77.8 %all-gather.5.cloned.1.call-start = ((), (), s32[]{:S(2)}) async-start(), calls=%async_computation.2 | async-start | bytes 8650752 | tf_op jit(solution)/shard_map/all_gather | solution.py:71
  9.2 204.3 %reduce-scatter.3.cloned.1.call-start = ((), (), s32[]{:S(2)}) async-start(), calls=%async_computation.3 | async-start | bytes 4718592 | tf_op jit(solution)/shard_map/reduce_scatter | solution.py:85
  12.6 2.3 copy-start.11
  12.6 2.5 copy-start.8
  108.1 5.5 copy-start.6
  123.7 89.7 %copy-start.5 = (bf16[256,256]{1,0:T(8,128)(2,1)S(1)}, bf16[256,256]{1,0:T(8,128)(2,1)}, u32[]{:S(2)}) copy-start(bf16[256,256]{1,0:T(8,128)(2,1)} %param.11) | copy-start | bytes 393220
  123.7 89.7 %copy-start.9 = (bf16[512,256]{1,0:T(8,128)(2,1)S(1)}, bf16[512,256]{1,0:T(8,128)(2,1)}, u32[]{:S(2)}) copy-start(bf16[512,256]{1,0:T(8,128)(2,1)} %param.13) | copy-start | bytes 786436
  123.7 89.7 %copy-start.10 = (f32[256]{0:T(256)S(1)}, f32[256]{0:T(256)}, u32[]{:S(2)}) copy-start(f32[256]{0:T(256)} %param.12) | copy-start | bytes 3076
  123.7 152.1 %all-gather.7.cloned.1.call-start = ((), (), s32[]{:S(2)}) async-start(), calls=%async_computation.4 | async-start | bytes 2359296 | tf_op jit(solution)/shard_map/all_gather | solution.py:97
  216.6 209.7 %reduce-scatter.5.cloned.1.call-start = ((), (), s32[]{:S(2)}) async-start(), calls=%async_computation.5 | async-start | bytes 8650752 | tf_op jit(solution)/shard_map/reduce_scatter | solution.py:123
  296.8 1.0 copy-start.4
  296.8 2.0 copy-start.2
  296.8 916.8 %all-gather.9.cloned.1.call-start = ((), (), s32[]{:S(2)}) async-start(), calls=%async_computation.6 | async-start | bytes 67371008 | tf_op jit(solution)/shard_map/all_gather | solution.py:99
  301.7 2.0 copy-start.7
  1213.7 21.8 %copy-start.1 = (bf16[1,32,1,128,128]{4,3,2,1,0:T(8,128)(2,1)S(1)}, bf16[1,32,1,128,128]{4,3,2,1,0:T(8,128)(2,1)}, u32[]{:S(2)}) copy-start(bf16[1,32,1,128,128]{4,3,2,1,0:T(8,128)(2,1)} %param.17) | copy-start | bytes 3145732
Sparse Core Ops, SparseCore 0:
  10.4 74.5 all-gather.4
  123.9 89.5 reduce-scatter.2
  216.7 59.0 all-gather.6
  297.0 129.2 reduce-scatter.4
  428.6 785.0 all-gather.8
